TPU v7x, 32 devices: a whole 2x2x4 slice. The times are simulated.
32 devices in a mesh: parts: 2 (over x), seq: 16 (over z, y, core).
Axes of the slice: x: 2, y: 2, z: 4, core: 2. Of those that a mesh axis runs over, the one named last changes fastest.
Arguments:
- prefix_latent: bfloat16 [61440, 512], P(('parts', 'seq')), parts along dimension 0, may hold values from -6 to 6
- block_order: int32 [480], P(('parts', 'seq')), parts along dimension 0, may hold values from 0 to 239, each once
- key_up: bfloat16 [512, 512], replicated, may hold values from -0.25 to 0.25
- value_up: bfloat16 [512, 512], replicated, may hold values from -0.25 to 0.25
- queries: bfloat16 [32, 4, 4096], P(('parts', 'seq')), parts along dimension 0, may hold values from -200 to 200
- new_keys: bfloat16 [32, 4, 512], P(('parts', 'seq')), parts along dimension 0, may hold values from -6 to 6
- new_values: bfloat16 [32, 4, 512], P(('parts', 'seq')), parts along dimension 0, may hold values from -6 to 6
- suffix_keys: bfloat16 [32, 4096, 512], P(('parts', 'seq')), parts along dimension 0, may hold values from -6 to 6
- suffix_values: bfloat16 [32, 4096, 512], P(('parts', 'seq')), parts along dimension 0, may hold values from -6 to 6
- suffix_len: int32 [32], P(('parts', 'seq')), parts along dimension 0, may hold values from 1 to 4096, 32768 in all
Outputs:
- attended: bfloat16 [32, 4, 4096], P(('parts', 'seq')), parts along dimension 0
There are 2 independent parts, one for each index of `parts`. A program takes and returns all parts, laid end to end along the dimension named above; an argument that names none is the same for every part. Nothing has to cross between parts.
Inputs may be any that keep to these rules, and one draw needn't show every extreme that they name: A request's cache holds its first suffix_len entries; some request holds exactly 4096. `block_order`: each block position appears once.
All inputs are finite; a program needn't handle non-finite values. No bound on the sum of `suffix_len` on one device may be relied on, other than what follows from the above.
Results may differ from a plain program's by a relative error of at most 0.005.
The roundings to bfloat16 on the way count: a program that leaves them out, or rounds other values in their place, can miss the bound.
Values may be sent and summed in bfloat16 or wider, within the bound.
No kernel may reach another device: no remote copies, remote signals or barrier semaphores. Data moves between devices by JAX's collectives and lax.ppermute only.
A program may use at most 128 MiB of HBM per device.

v0:
```python
import math
import jax
import jax.numpy as jnp
import numpy as np
from jax import lax
from jax.sharding import PartitionSpec as P

HD = 128
QH = 32
KVH = 4
BLK = 128
STEPS = 4
SUF = 4096


def phase_table(half):
    index = np.arange(half)
    freq = 500000.0 ** (-2.0 * index / (2 * half))
    mult = np.floor(2.0**24 * freq / (2 * np.pi)).astype(np.int64)
    return ((mult >> 12).astype(np.int32), (mult & 4095).astype(np.int32))


def rotate(values, position):
    half = values.shape[-1] // 2
    high, low = phase_table(half)
    spot = position[..., None]
    first = spot * jnp.asarray(low, dtype=jnp.int32)
    second = spot * jnp.asarray(high, dtype=jnp.int32) % 4096
    turns = (first + second * 4096) % 16777216
    angle = turns.astype(values.dtype) * (2.0 * math.pi / 16777216.0)
    cosine = jnp.cos(angle)[..., None, :]
    sine = jnp.sin(angle)[..., None, :]
    lower = values[..., :half]
    upper = values[..., half:]
    return jnp.concatenate([lower * cosine - upper * sine, upper * cosine + lower * sine], -1)


def local(
    prefix_latent,
    block_order,
    key_up,
    value_up,
    queries,
    new_keys,
    new_values,
    suffix_keys,
    suffix_values,
    suffix_len,
):
    seq_count = lax.axis_size("seq")
    pre_rows = prefix_latent.shape[0]
    prefix = pre_rows * seq_count
    req_rows = queries.shape[0]
    group = QH // KVH
    scale = 1.0 / math.sqrt(HD)
    rows = jnp.arange(pre_rows, dtype=jnp.int32)
    key_pos = jnp.repeat(block_order, BLK) * BLK + rows % BLK
    keys = jnp.dot(prefix_latent, key_up, preferred_element_type=jnp.float32).reshape(
        pre_rows, KVH, HD
    )
    keys = rotate(keys, key_pos).astype(jnp.bfloat16)
    values = (
        jnp.dot(prefix_latent, value_up, preferred_element_type=jnp.float32)
        .astype(jnp.bfloat16)
        .reshape(pre_rows, KVH, HD)
    )
    step_index = jnp.arange(STEPS, dtype=jnp.int32)
    query_pos = prefix + suffix_len[:, None] + step_index[None, :]
    query_rot = rotate(
        queries.astype(jnp.float32).reshape(req_rows, STEPS, QH, HD), query_pos
    ).astype(jnp.bfloat16)
    new_rot = rotate(
        new_keys.astype(jnp.float32).reshape(req_rows, STEPS, KVH, HD), query_pos
    ).astype(jnp.bfloat16)

    def shard_part(query_block):
        count = query_block.shape[0]
        width = query_block.shape[1]
        split = query_block.reshape(count, width, KVH, group, HD)
        scores = (
            jnp.einsum("rtkgd,pkd->rtkgp", split, keys, preferred_element_type=jnp.float32) * scale
        )
        peak = jnp.max(scores, -1)
        expo = jnp.exp(scores - peak[..., None])
        total = jnp.sum(expo, -1)
        summed = jnp.einsum(
            "rtkgp,pkd->rtkgd",
            expo.astype(jnp.bfloat16),
            values,
            preferred_element_type=jnp.float32,
        )
        part = summed / total[..., None]
        return (
            part.reshape(count, width, QH * HD),
            peak.reshape(count, width, QH),
            total.reshape(count, width, QH),
        )

    def prefix_attention(selected):
        width = selected.shape[1]
        whole = lax.all_gather(selected, "seq", axis=0, tiled=True)
        count = whole.shape[0]
        per_block = math.gcd(count, max(1, 512 // (width * QH)))
        blocks = whole.reshape(count // per_block, per_block, width, QH * HD)
        parts, peaks, totals = lax.map(shard_part, blocks)
        parts = parts.reshape(count, width, QH * HD)
        peaks = peaks.reshape(count, width, QH)
        totals = totals.reshape(count, width, QH)
        got_parts, got_peaks, got_totals = (
            lax.all_to_all(parts[:, None], "seq", split_axis=0, concat_axis=1, tiled=True),
            lax.all_to_all(peaks[:, None], "seq", split_axis=0, concat_axis=1, tiled=True),
            lax.all_to_all(totals[:, None], "seq", split_axis=0, concat_axis=1, tiled=True),
        )
        highest = jnp.max(got_peaks, 1)
        factor = got_totals * jnp.exp(got_peaks - highest[:, None])
        numer = jnp.sum(
            factor[..., None] * got_parts.reshape(req_rows, seq_count, width, QH, HD), 1
        )
        denom = jnp.sum(factor, 1)
        return (highest, numer, denom)

    flat_queries = query_rot.reshape(req_rows, STEPS, QH * HD)
    results = [prefix_attention(flat_queries[:, which : which + 1]) for which in range(STEPS)]
    highest = jnp.concatenate([entry[0] for entry in results], 1)
    numer = jnp.concatenate([entry[1] for entry in results], 1)
    denom = jnp.concatenate([entry[2] for entry in results], 1)
    split = query_rot.reshape(req_rows, STEPS, KVH, group, HD)
    cache_keys = suffix_keys.reshape(req_rows, SUF, KVH, HD)
    cache_values = suffix_values.reshape(req_rows, SUF, KVH, HD)
    cache_scores = (
        jnp.einsum("rtkgd,rpkd->rtkgp", split, cache_keys, preferred_element_type=jnp.float32)
        * scale
    )
    live = jnp.arange(SUF, dtype=jnp.int32)[None, :] < suffix_len[:, None]
    cache_scores = jnp.where(live[:, None, None, None, :], cache_scores, -jnp.inf)
    fresh_keys = new_rot.reshape(req_rows, STEPS, KVH, HD)
    fresh_values = new_values.reshape(req_rows, STEPS, KVH, HD)
    fresh_scores = (
        jnp.einsum("rtkgd,rukd->rtkgu", split, fresh_keys, preferred_element_type=jnp.float32)
        * scale
    )
    causal = step_index[:, None] >= step_index[None, :]
    fresh_scores = jnp.where(causal[None, :, None, None, :], fresh_scores, -jnp.inf)
    local_peak = jnp.maximum(jnp.max(cache_scores, -1), jnp.max(fresh_scores, -1))
    cache_exp = jnp.exp(cache_scores - local_peak[..., None])
    fresh_exp = jnp.exp(fresh_scores - local_peak[..., None])
    local_total = jnp.sum(cache_exp, -1) + jnp.sum(fresh_exp, -1)
    local_numer = jnp.einsum(
        "rtkgp,rpkd->rtkgd",
        cache_exp.astype(jnp.bfloat16),
        cache_values,
        preferred_element_type=jnp.float32,
    )
    local_numer = local_numer + jnp.einsum(
        "rtkgu,rukd->rtkgd",
        fresh_exp.astype(jnp.bfloat16),
        fresh_values,
        preferred_element_type=jnp.float32,
    )
    local_peak = local_peak.reshape(req_rows, STEPS, QH)
    local_total = local_total.reshape(req_rows, STEPS, QH)
    local_numer = local_numer.reshape(req_rows, STEPS, QH, HD)
    biggest = jnp.maximum(highest, local_peak)
    prefix_weight = jnp.exp(highest - biggest)
    local_weight = jnp.exp(local_peak - biggest)
    result = (numer * prefix_weight[..., None] + local_numer * local_weight[..., None]) / (
        denom * prefix_weight + local_total * local_weight
    )[..., None]
    return result.reshape(req_rows, STEPS, QH * HD).astype(jnp.bfloat16)


def solution(mesh):
    placed = (
        P(("parts", "seq"), None),
        P(("parts", "seq")),
        P(),
        P(),
        P(("parts", "seq"), None, None),
        P(("parts", "seq"), None, None),
        P(("parts", "seq"), None, None),
        P(("parts", "seq"), None, None),
        P(("parts", "seq"), None, None),
        P(("parts", "seq")),
    )
    return jax.shard_map(
        local,
        mesh=mesh,
        in_specs=placed,
        out_specs=P(("parts", "seq"), None, None),
        check_vma=False,
    )
```

profile of v0, /device:TPU:0, one launch (start us, length us, event | category | flops | bytes accessed | tf_op | source)
XLA Modules:
  0.0 271.2 jit_solution(17228398530204130083)
XLA Ops:
  3.2 23.8 %all_gather.12 = bf16[16,1,4096]{2,1,0:T(2,128)(2,1)S(1)} all-gather(bf16[1,1,4096]{2,1,0:T(2,128)(2,1)S(1)} %get-tuple-element.75), channel_id=1, replica_groups=mesh['parts'=2,'seq'=16] {'seq'}, dimensions={0}, use_global_device_ids=true | all-gather | bytes 139264 | tf_op jit(solution)/shard_map/all_gather | solution.py:101
  32.5 3.7 %copy.155 = f32[1920,4,64]{2,0,1:T(8,128)} copy(f32[1920,4,64]{0,2,1:T(8,128)} %get-tuple-element.72) | data formatting | bytes 3932160
  36.1 3.7 %copy.156 = f32[1920,4,64]{2,0,1:T(8,128)} copy(f32[1920,4,64]{0,2,1:T(8,128)} %get-tuple-element.71) | data formatting | bytes 3932160
  39.9 4.3 %fusion.77 = (f32[1920,64]{1,0:T(8,128)S(1)}, f32[1920,64]{1,0:T(8,128)S(1)}) fusion(s32[64]{0:T(128)S(1)} %copy-done.20, s32[64]{0:T(128)S(1)} %copy-done.19, s32[1920]{0:T(1024)S(1)} %fusion.96), kind=kLoop, calls=%fused_computation.80 | loop fusion | flops 3440640 | bytes 991232 | tf_op jit(solution)/shard_map/cos | solution.py:31
  44.3 4.5 %subtract_convert_fusion = (bf16[1920,4,64]{2,0,1:T(8,128)(2,1)S(1)}, bf16[1920,4,64]{2,0,1:T(8,128)(2,1)S(1)}) fusion(f32[1920,4,64]{2,0,1:T(8,128)} %copy.156, f32[1920,4,64]{2,0,1:T(8,128)} %copy.155, f32[1920,64]{1,0:T(8,128)S(1)} %get-tuple-element.89, f32[1920,64]{1,0:T(8,128)S(1)} %get-tuple-element.88), kind=kLoop, calls=%fused_computation.20 | loop fusion | flops 3932160 | bytes 6881280 | tf_op jit(solution)/shard_map/convert.12
  54.4 3.7 %all-to-all-start = ((f32[16,1,1,32]{3,2,1,0:T(1,128)}), f32[16,1,1,32]{3,2,1,0:T(1,128)S(1)}, u32[]{:S(2)}, u32[]{:S(2)}) async-start(f32[16,1,1,32]{3,2,1,0:T(1,128)} %copy.101), calls=%async_computation | async-start | bytes 16384 | tf_op jit(solution)/shard_map/all_to_all | solution.py:112
  61.1 22.2 %all_gather.13 = bf16[16,1,4096]{2,1,0:T(2,128)(2,1)S(1)} all-gather(bf16[1,1,4096]{2,1,0:T(2,128)(2,1)S(1)} %get-tuple-element.85), channel_id=1, replica_groups=mesh['parts'=2,'seq'=16] {'seq'}, dimensions={0}, use_global_device_ids=true | all-gather | bytes 139264 | tf_op jit(solution)/shard_map/all_gather | solution.py:101
  87.2 18.2 %all_gather.14 = bf16[16,1,4096]{2,1,0:T(2,128)(2,1)S(1)} all-gather(bf16[1,1,4096]{2,1,0:T(2,128)(2,1)S(1)} %get-tuple-element.84), channel_id=1, replica_groups=mesh['parts'=2,'seq'=16] {'seq'}, dimensions={0}, use_global_device_ids=true | all-gather | bytes 139264 | tf_op jit(solution)/shard_map/all_gather | solution.py:101
  109.4 19.5 %all_gather.15 = bf16[16,1,4096]{2,1,0:T(2,128)(2,1)S(1)} all-gather(bf16[1,1,4096]{2,1,0:T(2,128)(2,1)S(1)} %get-tuple-element.76), channel_id=1, replica_groups=mesh['parts'=2,'seq'=16] {'seq'}, dimensions={0}, use_global_device_ids=true | all-gather | bytes 139264 | tf_op jit(solution)/shard_map/all_gather | solution.py:101
  133.5 6.9 %reshape.1695 = bf16[4096,4,128]{2,1,0:T(4,128)(2,1)} reshape(bf16[1,4096,512]{2,1,0:T(8,128)(2,1)} %param.23) | data formatting | bytes 8388608 | tf_op jit(solution)/shard_map/reshape.165
  140.4 3.8 %all-to-all-start.1 = ((f32[16,1,1,32]{3,2,1,0:T(1,128)}), f32[16,1,1,32]{3,2,1,0:T(1,128)S(1)}, u32[]{:S(2)}, u32[]{:S(2)}) async-start(f32[16,1,1,32]{3,2,1,0:T(1,128)} %copy.102), calls=%async_computation.1 | async-start | bytes 16384 | tf_op jit(solution)/shard_map/all_to_all | solution.py:111
  144.2 3.8 %fusion.125 = (f32[4,4,8]{2,0,1:T(4,128)S(1)}, f32[1,4,4,8,4096]{4,3,1,2,0:T(8,128)S(1)}) fusion(bf16[4096,4,128,1]{2,1,0,3:T(4,128)(2,1)} %bitcast.286, pred[4096]{0:T(1024)(128)(4,1)S(1)} %iota_compare_fusion, bf16[4,4,8,64]{3,2,1,0:T(8,128)(2,1)S(1)} %bitcast.301, bf16[4,4,8,64]{3,2,1,0:T(8,128)(2,1)S(1)} %bitcast.299), kind=kOutput, calls=%fused_computation.167 | convolution fusion | flops 135856000 | bytes 6328832 | tf_op jit(solution)/shard_map/rtkgd,rpkd->rtkgp/dot_general | solution.py:131
  150.6 4.1 %all-to-all-start.3 = ((f32[16,1,1,32]{3,2,1,0:T(1,128)}), f32[16,1,1,32]{3,2,1,0:T(1,128)S(1)}, u32[]{:S(2)}, u32[]{:S(2)}) async-start(f32[16,1,1,32]{3,2,1,0:T(1,128)} %copy.107), calls=%async_computation.3 | async-start | bytes 16384 | tf_op jit(solution)/shard_map/all_to_all | solution.py:112
  155.4 5.6 %all-to-all-done.3 = f32[16,1,1,32]{3,2,1,0:T(1,128)S(1)} async-done(((f32[16,1,1,32]{3,2,1,0:T(1,128)}), f32[16,1,1,32]{3,2,1,0:T(1,128)S(1)}, u32[]{:S(2)}, u32[]{:S(2)}) %all-to-all-start.3) | async-done | bytes 2080 | tf_op jit(solution)/shard_map/all_to_all | solution.py:112
  161.0 3.5 %all-to-all-start.4 = ((f32[16,1,1,32]{3,2,1,0:T(1,128)}), f32[16,1,1,32]{3,2,1,0:T(1,128)S(1)}, u32[]{:S(2)}, u32[]{:S(2)}) async-start(f32[16,1,1,32]{3,2,1,0:T(1,128)} %copy.108), calls=%async_computation.4 | async-start | bytes 16384 | tf_op jit(solution)/shard_map/all_to_all | solution.py:111
  165.3 5.6 %all-to-all-done.4 = f32[16,1,1,32]{3,2,1,0:T(1,128)S(1)} async-done(((f32[16,1,1,32]{3,2,1,0:T(1,128)}), f32[16,1,1,32]{3,2,1,0:T(1,128)S(1)}, u32[]{:S(2)}, u32[]{:S(2)}) %all-to-all-start.4) | async-done | bytes 2080 | tf_op jit(solution)/shard_map/all_to_all | solution.py:111
  170.9 3.5 %all-to-all-start.6 = ((f32[16,1,1,32]{3,2,1,0:T(1,128)}), f32[16,1,1,32]{3,2,1,0:T(1,128)S(1)}, u32[]{:S(2)}, u32[]{:S(2)}) async-start(f32[16,1,1,32]{3,2,1,0:T(1,128)} %copy.113), calls=%async_computation.6 | async-start | bytes 16384 | tf_op jit(solution)/shard_map/all_to_all | solution.py:112
  175.1 5.6 %all-to-all-done.6 = f32[16,1,1,32]{3,2,1,0:T(1,128)S(1)} async-done(((f32[16,1,1,32]{3,2,1,0:T(1,128)}), f32[16,1,1,32]{3,2,1,0:T(1,128)S(1)}, u32[]{:S(2)}, u32[]{:S(2)}) %all-to-all-start.6) | async-done | bytes 2080 | tf_op jit(solution)/shard_map/all_to_all | solution.py:112
  181.3 3.5 %all-to-all-start.7 = ((f32[16,1,1,32]{3,2,1,0:T(1,128)}), f32[16,1,1,32]{3,2,1,0:T(1,128)S(1)}, u32[]{:S(2)}, u32[]{:S(2)}) async-start(f32[16,1,1,32]{3,2,1,0:T(1,128)} %copy.114), calls=%async_computation.7 | async-start | bytes 16384 | tf_op jit(solution)/shard_map/all_to_all | solution.py:111
  185.8 6.9 %reshape.1699 = bf16[4096,4,128]{2,1,0:T(4,128)(2,1)} reshape(bf16[1,4096,512]{2,1,0:T(8,128)(2,1)} %param.24) | data formatting | bytes 8388608 | tf_op jit(solution)/shard_map/reshape.180
  192.7 6.0 %all-to-all-start.9 = ((f32[16,1,1,32]{3,2,1,0:T(1,128)}), f32[16,1,1,32]{3,2,1,0:T(1,128)S(1)}, u32[]{:S(2)}, u32[]{:S(2)}) async-start(f32[16,1,1,32]{3,2,1,0:T(1,128)} %copy.119), calls=%async_computation.9 | async-start | bytes 16384 | tf_op jit(solution)/shard_map/all_to_all | solution.py:112
  198.7 3.0 %fusion.3 = f32[4,4,8,128]{3,2,1,0:T(8,128)S(1)} fusion(bf16[4096,4,128,1]{2,1,0,3:T(4,128)(2,1)} %bitcast.285, f32[1,4,4,8,4096]{4,3,1,2,0:T(8,128)S(1)} %get-tuple-element.117, f32[4,4,8]{2,0,1:T(4,128)S(1)} %max.48), kind=kOutput, calls=%fused_computation.4 | convolution fusion | flops 135266304 | bytes 6357504 | tf_op jit(solution)/shard_map/rtkgp,rpkd->rtkgd/dot_general | solution.py:148
  205.7 3.5 %all-to-all-start.10 = ((f32[16,1,1,32]{3,2,1,0:T(1,128)}), f32[16,1,1,32]{3,2,1,0:T(1,128)S(1)}, u32[]{:S(2)}, u32[]{:S(2)}) async-start(f32[16,1,1,32]{3,2,1,0:T(1,128)} %copy.120), calls=%async_computation.10 | async-start | bytes 16384 | tf_op jit(solution)/shard_map/all_to_all | solution.py:111
  210.4 5.1 %all-to-all-done.10 = f32[16,1,1,32]{3,2,1,0:T(1,128)S(1)} async-done(((f32[16,1,1,32]{3,2,1,0:T(1,128)}), f32[16,1,1,32]{3,2,1,0:T(1,128)S(1)}, u32[]{:S(2)}, u32[]{:S(2)}) %all-to-all-start.10) | async-done | bytes 2080 | tf_op jit(solution)/shard_map/all_to_all | solution.py:111
  215.5 3.5 %all-to-all-start.2 = ((f32[16,1,1,4096]{3,1,2,0:T(1,128)}), f32[16,1,1,4096]{3,1,2,0:T(1,128)S(1)}, u32[]{:S(2)}, u32[]{:S(2)}) async-start(f32[16,1,1,4096]{3,1,2,0:T(1,128)} %bitcast.19), calls=%async_computation.2 | async-start | bytes 524288 | tf_op jit(solution)/shard_map/all_to_all | solution.py:110
  222.1 7.0 %all-to-all-done.2 = f32[16,1,1,4096]{3,1,2,0:T(1,128)S(1)} async-done(((f32[16,1,1,4096]{3,1,2,0:T(1,128)}), f32[16,1,1,4096]{3,1,2,0:T(1,128)S(1)}, u32[]{:S(2)}, u32[]{:S(2)}) %all-to-all-start.2) | async-done | bytes 262176 | tf_op jit(solution)/shard_map/all_to_all | solution.py:110
  229.1 3.5 %all-to-all-start.5 = ((f32[16,1,1,4096]{3,1,2,0:T(1,128)}), f32[16,1,1,4096]{3,1,2,0:T(1,128)S(1)}, u32[]{:S(2)}, u32[]{:S(2)}) async-start(f32[16,1,1,4096]{3,1,2,0:T(1,128)} %bitcast.35), calls=%async_computation.5 | async-start | bytes 524288 | tf_op jit(solution)/shard_map/all_to_all | solution.py:110
  233.4 9.3 %all-to-all-done.5 = f32[16,1,1,4096]{3,1,2,0:T(1,128)S(1)} async-done(((f32[16,1,1,4096]{3,1,2,0:T(1,128)}), f32[16,1,1,4096]{3,1,2,0:T(1,128)S(1)}, u32[]{:S(2)}, u32[]{:S(2)}) %all-to-all-start.5) | async-done | bytes 262176 | tf_op jit(solution)/shard_map/all_to_all | solution.py:110
  242.6 3.5 %all-to-all-start.8 = ((f32[16,1,1,4096]{3,1,2,0:T(1,128)}), f32[16,1,1,4096]{3,1,2,0:T(1,128)S(1)}, u32[]{:S(2)}, u32[]{:S(2)}) async-start(f32[16,1,1,4096]{3,1,2,0:T(1,128)} %bitcast.50), calls=%async_computation.8 | async-start | bytes 524288 | tf_op jit(solution)/shard_map/all_to_all | solution.py:110
  247.6 8.6 %all-to-all-done.8 = f32[16,1,1,4096]{3,1,2,0:T(1,128)S(1)} async-done(((f32[16,1,1,4096]{3,1,2,0:T(1,128)}), f32[16,1,1,4096]{3,1,2,0:T(1,128)S(1)}, u32[]{:S(2)}, u32[]{:S(2)}) %all-to-all-start.8) | async-done | bytes 262176 | tf_op jit(solution)/shard_map/all_to_all | solution.py:110
  256.2 3.5 %all-to-all-start.11 = ((f32[16,1,1,4096]{3,1,2,0:T(1,128)}), f32[16,1,1,4096]{3,1,2,0:T(1,128)S(1)}, u32[]{:S(2)}, u32[]{:S(2)}) async-start(f32[16,1,1,4096]{3,1,2,0:T(1,128)} %bitcast.65), calls=%async_computation.11 | async-start | bytes 524288 | tf_op jit(solution)/shard_map/all_to_all | solution.py:110
  261.0 8.7 %all-to-all-done.11 = f32[16,1,1,4096]{3,1,2,0:T(1,128)S(1)} async-done(((f32[16,1,1,4096]{3,1,2,0:T(1,128)}), f32[16,1,1,4096]{3,1,2,0:T(1,128)S(1)}, u32[]{:S(2)}, u32[]{:S(2)}) %all-to-all-start.11) | async-done | bytes 262176 | tf_op jit(solution)/shard_map/all_to_all | solution.py:110
  (145 shorter events, 48.3 us)
Async XLA Ops:
  0.0 27.7 %copy-start = (bf16[1920,512]{1,0:T(8,128)(2,1)S(1)}, bf16[1920,512]{1,0:T(8,128)(2,1)}, u32[]{:S(2)}) copy-start(bf16[1920,512]{1,0:T(8,128)(2,1)} %param.16) | copy-start | bytes 5898244
  36.1 3.7 %copy-start.22 = (s32[15]{0:T(128)S(1)}, s32[15]{0:T(128)}, u32[]{:S(2)}) copy-start(s32[15]{0:T(128)} %param.17) | copy-start | bytes 184
  36.1 3.8 %copy-start.19 = (s32[64]{0:T(128)S(1)}, s32[64]{0:T(128)}, u32[]{:S(2)}) copy-start(s32[64]{0:T(128)} %constant.146.clone) | copy-start | bytes 772
  36.1 3.8 %copy-start.20 = (s32[64]{0:T(128)S(1)}, s32[64]{0:T(128)}, u32[]{:S(2)}) copy-start(s32[64]{0:T(128)} %constant.147.clone) | copy-start | bytes 772
  51.1 1.9 copy-start.4
  51.1 7.0 %copy-start.21 = (bf16[512,512]{1,0:T(8,128)(2,1)S(1)}, bf16[512,512]{1,0:T(8,128)(2,1)}, u32[]{:S(2)}) copy-start(bf16[512,512]{1,0:T(8,128)(2,1)} %param.19) | copy-start | bytes 1572868
  54.4 86.0 %all-to-all-start = ((f32[16,1,1,32]{3,2,1,0:T(1,128)}), f32[16,1,1,32]{3,2,1,0:T(1,128)S(1)}, u32[]{:S(2)}, u32[]{:S(2)}) async-start(f32[16,1,1,32]{3,2,1,0:T(1,128)} %copy.101), calls=%async_computation | async-start | bytes 16384 | tf_op jit(solution)/shard_map/all_to_all | solution.py:112
  58.1 2.1 copy-start.5
  59.4 1.7 copy-start.23
  59.4 24.6 %copy-start.3 = (bf16[1920,4,128,1]{2,0,3,1:T(8,128)(2,1)S(1)}, bf16[1920,4,128,1]{2,0,3,1:T(8,128)(2,1)}, u32[]{:S(2)}) copy-start(bf16[1920,4,128,1]{2,0,3,1:T(8,128)(2,1)} %copy-done.2) | copy-start | bytes 5898244
  84.8 1.5 copy-start.24
  86.4 20.6 %copy-start.11 = (f32[16,4,8]{0,2,1:T(8,128)}, f32[16,4,8]{0,2,1:T(8,128)S(1)}, u32[]{:S(2)}) copy-start(f32[16,4,8]{0,2,1:T(8,128)S(1)} %fusion.13) | copy-start | bytes 6148
  140.4 7.6 %copy-start.12 = (f32[16,4,8]{0,2,1:T(8,128)S(1)}, f32[16,4,8]{0,2,1:T(8,128)}, u32[]{:S(2)}) copy-start(f32[16,4,8]{0,2,1:T(8,128)} %copy-done.11) | copy-start | bytes 6148
  140.4 14.3 %copy-start.17 = (bf16[1,4,512]{2,1,0:T(4,128)(2,1)S(1)}, bf16[1,4,512]{2,1,0:T(4,128)(2,1)}, u32[]{:S(2)}) copy-start(bf16[1,4,512]{2,1,0:T(4,128)(2,1)} %param.21) | copy-start | bytes 12292
  140.4 24.1 %copy-start.14 = (f32[4,64]{1,0:T(4,128)S(1)}, f32[4,64]{1,0:T(4,128)}, u32[]{:S(2)}) copy-start(f32[4,64]{1,0:T(4,128)} %copy-done.13) | copy-start | bytes 3076
  140.4 24.1 %copy-start.16 = (f32[4,64]{1,0:T(4,128)S(1)}, f32[4,64]{1,0:T(4,128)}, u32[]{:S(2)}) copy-start(f32[4,64]{1,0:T(4,128)} %copy-done.15) | copy-start | bytes 3076
  140.4 10.2 %all-to-all-start.1 = ((f32[16,1,1,32]{3,2,1,0:T(1,128)}), f32[16,1,1,32]{3,2,1,0:T(1,128)S(1)}, u32[]{:S(2)}, u32[]{:S(2)}) async-start(f32[16,1,1,32]{3,2,1,0:T(1,128)} %copy.102), calls=%async_computation.1 | async-start | bytes 16384 | tf_op jit(solution)/shard_map/all_to_all | solution.py:111
  150.6 10.4 %all-to-all-start.3 = ((f32[16,1,1,32]{3,2,1,0:T(1,128)}), f32[16,1,1,32]{3,2,1,0:T(1,128)S(1)}, u32[]{:S(2)}, u32[]{:S(2)}) async-start(f32[16,1,1,32]{3,2,1,0:T(1,128)} %copy.107), calls=%async_computation.3 | async-start | bytes 16384 | tf_op jit(solution)/shard_map/all_to_all | solution.py:112
  161.0 23.7 %copy-start.6 = (f32[16,1,1,32]{3,2,1,0:T(1,128)}, f32[16,1,1,32]{3,2,1,0:T(1,128)S(1)}, u32[]{:S(2)}) copy-start(f32[16,1,1,32]{3,2,1,0:T(1,128)S(1)} %all-to-all-done.3) | copy-start | bytes 6148
  161.0 9.9 %all-to-all-start.4 = ((f32[16,1,1,32]{3,2,1,0:T(1,128)}), f32[16,1,1,32]{3,2,1,0:T(1,128)S(1)}, u32[]{:S(2)}, u32[]{:S(2)}) async-start(f32[16,1,1,32]{3,2,1,0:T(1,128)} %copy.108), calls=%async_computation.4 | async-start | bytes 16384 | tf_op jit(solution)/shard_map/all_to_all | solution.py:111
  170.9 9.8 %all-to-all-start.6 = ((f32[16,1,1,32]{3,2,1,0:T(1,128)}), f32[16,1,1,32]{3,2,1,0:T(1,128)S(1)}, u32[]{:S(2)}, u32[]{:S(2)}) async-start(f32[16,1,1,32]{3,2,1,0:T(1,128)} %copy.113), calls=%async_computation.6 | async-start | bytes 16384 | tf_op jit(solution)/shard_map/all_to_all | solution.py:112
  181.3 11.5 %all-to-all-start.7 = ((f32[16,1,1,32]{3,2,1,0:T(1,128)}), f32[16,1,1,32]{3,2,1,0:T(1,128)S(1)}, u32[]{:S(2)}, u32[]{:S(2)}) async-start(f32[16,1,1,32]{3,2,1,0:T(1,128)} %copy.114), calls=%async_computation.7 | async-start | bytes 16384 | tf_op jit(solution)/shard_map/all_to_all | solution.py:111
  192.7 12.3 %all-to-all-start.9 = ((f32[16,1,1,32]{3,2,1,0:T(1,128)}), f32[16,1,1,32]{3,2,1,0:T(1,128)S(1)}, u32[]{:S(2)}, u32[]{:S(2)}) async-start(f32[16,1,1,32]{3,2,1,0:T(1,128)} %copy.119), calls=%async_computation.9 | async-start | bytes 16384 | tf_op jit(solution)/shard_map/all_to_all | solution.py:112
  201.8 19.9 %copy-start.18 = (bf16[1,4,512]{2,1,0:T(4,128)(2,1)S(1)}, bf16[1,4,512]{2,1,0:T(4,128)(2,1)}, u32[]{:S(2)}) copy-start(bf16[1,4,512]{2,1,0:T(4,128)(2,1)} %param.22) | copy-start | bytes 12292
  201.8 20.3 %copy-start.7 = (f32[16,1,1,32]{3,2,1,0:T(1,128)S(1)}, f32[16,1,1,32]{3,2,1,0:T(1,128)}, u32[]{:S(2)}) copy-start(f32[16,1,1,32]{3,2,1,0:T(1,128)} %copy-done.6) | copy-start | bytes 6148
  201.8 20.3 %copy-start.9 = (f32[16,1,1,32]{3,2,1,0:T(1,128)S(1)}, f32[16,1,1,32]{3,2,1,0:T(1,128)}, u32[]{:S(2)}) copy-start(f32[16,1,1,32]{3,2,1,0:T(1,128)} %copy-done.8) | copy-start | bytes 6148
  205.7 9.9 %all-to-all-start.10 = ((f32[16,1,1,32]{3,2,1,0:T(1,128)}), f32[16,1,1,32]{3,2,1,0:T(1,128)S(1)}, u32[]{:S(2)}, u32[]{:S(2)}) async-start(f32[16,1,1,32]{3,2,1,0:T(1,128)} %copy.120), calls=%async_computation.10 | async-start | bytes 16384 | tf_op jit(solution)/shard_map/all_to_all | solution.py:111
  215.5 13.5 %all-to-all-start.2 = ((f32[16,1,1,4096]{3,1,2,0:T(1,128)}), f32[16,1,1,4096]{3,1,2,0:T(1,128)S(1)}, u32[]{:S(2)}, u32[]{:S(2)}) async-start(f32[16,1,1,4096]{3,1,2,0:T(1,128)} %bitcast.19), calls=%async_computation.2 | async-start | bytes 524288 | tf_op jit(solution)/shard_map/all_to_all | solution.py:110
  219.1 52.2 %copy-start.1 = (bf16[1920,512]{1,0:T(8,128)(2,1)S(1)}, bf16[1920,512]{1,0:T(8,128)(2,1)}, u32[]{:S(2)}) copy-start(bf16[1920,512]{1,0:T(8,128)(2,1)} %param.16) | copy-start | bytes 5898244
  229.1 13.5 %all-to-all-start.5 = ((f32[16,1,1,4096]{3,1,2,0:T(1,128)}), f32[16,1,1,4096]{3,1,2,0:T(1,128)S(1)}, u32[]{:S(2)}, u32[]{:S(2)}) async-start(f32[16,1,1,4096]{3,1,2,0:T(1,128)} %bitcast.35), calls=%async_computation.5 | async-start | bytes 524288 | tf_op jit(solution)/shard_map/all_to_all | solution.py:110
  242.6 13.5 %all-to-all-start.8 = ((f32[16,1,1,4096]{3,1,2,0:T(1,128)}), f32[16,1,1,4096]{3,1,2,0:T(1,128)S(1)}, u32[]{:S(2)}, u32[]{:S(2)}) async-start(f32[16,1,1,4096]{3,1,2,0:T(1,128)} %bitcast.50), calls=%async_computation.8 | async-start | bytes 524288 | tf_op jit(solution)/shard_map/all_to_all | solution.py:110
  256.2 13.5 %all-to-all-start.11 = ((f32[16,1,1,4096]{3,1,2,0:T(1,128)}), f32[16,1,1,4096]{3,1,2,0:T(1,128)S(1)}, u32[]{:S(2)}, u32[]{:S(2)}) async-start(f32[16,1,1,4096]{3,1,2,0:T(1,128)} %bitcast.65), calls=%async_computation.11 | async-start | bytes 524288 | tf_op jit(solution)/shard_map/all_to_all | solution.py:110
  (7 other events, 6.7 us)
where the time goes:
time: 273 us; the launch traced here: 271 us
  blocking collectives  83.6 us (31%)
  waiting for transfers between devices  59.9 us (22%)
  starting transfers between devices  45.6 us (17%)
  local copies, waits for them, and re-layouts  40.9 us (15%)
  other arithmetic  22.1 us (8%)
  matrix products  17.6 us (6%)
    all_gather x4, blocking collectives, prefix_attention(): whole = lax.all_gather(selected, 'seq', axis=0, tiled=True)  83.6 us
    all_to_all x4, waiting for transfers between devices, prefix_attention(): lax.all_to_all(parts[:, None], 'seq', split_axis=0, concat_axis=1, tiled=...  33.5 us
    all_to_all x4, starting transfers between devices, prefix_attention(): lax.all_to_all(totals[:, None], 'seq', split_axis=0, concat_axis=1, tiled...  17.2 us
    unnamed x61, local copies, waits for them, and re-layouts  14.6 us
    all_to_all x4, starting transfers between devices, prefix_attention(): lax.all_to_all(peaks[:, None], 'seq', split_axis=0, concat_axis=1, tiled=...  14.3 us
    all_to_all x4, starting transfers between devices, prefix_attention(): lax.all_to_all(parts[:, None], 'seq', split_axis=0, concat_axis=1, tiled=...  14.1 us
    another operation x2, local copies, waits for them, and re-layouts  13.9 us
    all_to_all x4, waiting for transfers between devices, prefix_attention(): lax.all_to_all(totals[:, None], 'seq', split_axis=0, concat_axis=1, tiled...  13.8 us
  transfers between devices with their start and end apart: 12, of which 10 were waited for; matrix products, arithmetic and copies ran while one was open for 17% of the time, Pallas kernels for 0%

commit v1 on v0

--- a/solution.py
+++ b/solution.py
@@ -108,7 +108,12 @@
         totals = totals.reshape(count, width, QH)
         got_parts, got_peaks, got_totals = (
             lax.all_to_all(parts[:, None], "seq", split_axis=0, concat_axis=1, tiled=True),
-            lax.all_to_all(peaks[:, None], "seq", split_axis=0, concat_axis=1, tiled=True),
+            jnp.concatenate(
+                lax.all_to_all(
+                    jnp.stack(jnp.split(peaks[:, None], lax.axis_size("seq"), axis=0)), "seq", 0, 0
+                ),
+                axis=1,
+            ),
             lax.all_to_all(totals[:, None], "seq", split_axis=0, concat_axis=1, tiled=True),
         )
         highest = jnp.max(got_peaks, 1)

time: 273 us -> 336 us (1.23)
  local copies, waits for them, and re-layouts: 40.9 us -> 75.7 us
  matrix products: 17.6 us -> 34.4 us
  other arithmetic: 22.1 us -> 33.1 us
    unnamed x61 -> x153, local copies, waits for them, and re-layouts: 14.6 us -> 33.2 us
    another operation x6 -> x70, local copies, waits for them, and re-layouts: 16.5 us -> 31.5 us  [the longest x68 17.7 us: prefix_attention(): jnp.stack(jnp.split(peaks[:, None], lax.axis_size('seq'), axis=0))]
    reduce_sum x4, other arithmetic: 3.1 us -> 12 us  [shard_part(): total = jnp.sum(expo, -1)]
    dot_general x4, matrix products: 3.18 us -> 12 us  [shard_part(): jnp.einsum('rtkgd,pkd->rtkgp', split, keys, preferred_element_type=jnp.fl...]
    dot_general x4, matrix products: 3.38 us -> 8.19 us  [shard_part(): jnp.einsum('rtkgp,pkd->rtkgd', expo.astype(jnp.bfloat16), values, preferr...]
  transfers between devices with their start and end apart: 12 -> 12, of which waited for: 10 -> 10; matrix products, arithmetic and copies ran while one was open for 17% -> 31% of each run, Pallas kernels for 0% -> 0%
where the time goes in v1:
time: 336 us; the launch traced here: 334 us
  blocking collectives  83.9 us (25%)
  local copies, waits for them, and re-layouts  75.7 us (23%)
  waiting for transfers between devices  60.7 us (18%)
  starting transfers between devices  45 us (13%)
  matrix products  34.4 us (10%)
  other arithmetic  33.1 us (10%)
    all_gather x4, blocking collectives, prefix_attention(): whole = lax.all_gather(selected, 'seq', axis=0, tiled=True)  83.9 us
    all_to_all x4, waiting for transfers between devices, prefix_attention(): lax.all_to_all(parts[:, None], 'seq', split_axis=0, concat_axis=1, tiled=...  33.5 us
    unnamed x153, local copies, waits for them, and re-layouts  33.2 us
    another operation x68, local copies, waits for them, and re-layouts, prefix_attention(): jnp.stack(jnp.split(peaks[:, None], lax.axis_size('seq'), axis=0))  17.7 us
    all_to_all x4, starting transfers between devices, prefix_attention(): lax.all_to_all(jnp.stack(jnp.split(peaks[:, None], lax.axis_size('seq'),...  16.5 us
    all_to_all x4, waiting for transfers between devices, prefix_attention(): lax.all_to_all(totals[:, None], 'seq', split_axis=0, concat_axis=1, tiled...  15.1 us
    all_to_all x4, starting transfers between devices, prefix_attention(): lax.all_to_all(totals[:, None], 'seq', split_axis=0, concat_axis=1, tiled...  14.4 us
    all_to_all x4, starting transfers between devices, prefix_attention(): lax.all_to_all(parts[:, None], 'seq', split_axis=0, concat_axis=1, tiled=...  14.1 us
  transfers between devices with their start and end apart: 12, of which 10 were waited for; matrix products, arithmetic and copies ran while one was open for 31% of the time, Pallas kernels for 0%

profile of v1, /device:TPU:0, one launch (start us, length us, event | category | flops | bytes accessed | tf_op | source)
XLA Modules:
  0.0 334.4 jit_solution(5839990708131028572)
XLA Ops:
  2.7 23.8 %all_gather.12 = bf16[16,1,4096]{2,1,0:T(2,128)(2,1)S(1)} all-gather(bf16[1,1,4096]{2,1,0:T(2,128)(2,1)S(1)} %get-tuple-element.162), channel_id=1, replica_groups=mesh['parts'=2,'seq'=16] {'seq'}, dimensions={0}, use_global_device_ids=true | all-gather | bytes 139264 | tf_op jit(solution)/shard_map/all_gather | solution.py:101
  32.0 3.7 %copy.219 = f32[1920,4,64]{2,0,1:T(8,128)} copy(f32[1920,4,64]{0,2,1:T(8,128)} %get-tuple-element.159) | data formatting | bytes 3932160
  35.6 3.7 %copy.220 = f32[1920,4,64]{2,0,1:T(8,128)} copy(f32[1920,4,64]{0,2,1:T(8,128)} %get-tuple-element.158) | data formatting | bytes 3932160
  39.4 4.3 %fusion.77 = (f32[1920,64]{1,0:T(8,128)S(1)}, f32[1920,64]{1,0:T(8,128)S(1)}) fusion(s32[64]{0:T(128)S(1)} %copy-done.18, s32[64]{0:T(128)S(1)} %copy-done.17, s32[1920]{0:T(1024)S(1)} %fusion.96), kind=kLoop, calls=%fused_computation.80 | loop fusion | flops 3440640 | bytes 991232 | tf_op jit(solution)/shard_map/cos | solution.py:31
  43.8 4.5 %subtract_convert_fusion = (bf16[1920,4,64]{2,0,1:T(8,128)(2,1)S(1)}, bf16[1920,4,64]{2,0,1:T(8,128)(2,1)S(1)}) fusion(f32[1920,4,64]{2,0,1:T(8,128)} %copy.220, f32[1920,4,64]{2,0,1:T(8,128)} %copy.219, f32[1920,64]{1,0:T(8,128)S(1)} %get-tuple-element.169, f32[1920,64]{1,0:T(8,128)S(1)} %get-tuple-element.168), kind=kLoop, calls=%fused_computation.20 | loop fusion | flops 3932160 | bytes 6881280 | tf_op jit(solution)/shard_map/convert.12
  62.2 3.6 %all-to-all-start.1 = ((f32[16,1,1,1,32]{4,3,2,1,0:T(1,128)}), f32[16,1,1,1,32]{4,3,2,1,0:T(1,128)S(1)}, u32[]{:S(2)}, u32[]{:S(2)}) async-start(f32[16,1,1,1,32]{4,3,2,1,0:T(1,128)} %constant_dynamic-update-slice_fusion), calls=%async_computation.1 | async-start | bytes 16384 | tf_op jit(solution)/shard_map/all_to_all | solution.py:112
  71.8 22.2 %all_gather.13 = bf16[16,1,4096]{2,1,0:T(2,128)(2,1)S(1)} all-gather(bf16[1,1,4096]{2,1,0:T(2,128)(2,1)S(1)} %get-tuple-element.165), channel_id=1, replica_groups=mesh['parts'=2,'seq'=16] {'seq'}, dimensions={0}, use_global_device_ids=true | all-gather | bytes 139264 | tf_op jit(solution)/shard_map/all_gather | solution.py:101
  94.8 4.2 %bitcast_reduce_fusion.2 = (f32[16,4,8]{0,2,1:T(8,128)S(1)}, f32[4,1920,16,8]{1,2,3,0:T(8,128)}) fusion(bf16[1920,4,128,1]{2,0,3,1:T(8,128)(2,1)} %copy-done.2, bf16[16,4,8,128]{3,2,1,0:T(8,128)(2,1)S(1)} %bitcast.289), kind=kOutput, calls=%fused_computation.14 | convolution fusion | flops 253623808 | bytes 6031360 | tf_op jit(solution)/shard_map/while/body/eval_jaxpr/rtkgd,pkd->rtkgp/dot_general | solution.py:81
  110.9 18.2 %all_gather.14 = bf16[16,1,4096]{2,1,0:T(2,128)(2,1)S(1)} all-gather(bf16[1,1,4096]{2,1,0:T(2,128)(2,1)S(1)} %get-tuple-element.164), channel_id=1, replica_groups=mesh['parts'=2,'seq'=16] {'seq'}, dimensions={0}, use_global_device_ids=true | all-gather | bytes 139264 | tf_op jit(solution)/shard_map/all_gather | solution.py:101
  147.9 19.7 %all_gather.15 = bf16[16,1,4096]{2,1,0:T(2,128)(2,1)S(1)} all-gather(bf16[1,1,4096]{2,1,0:T(2,128)(2,1)S(1)} %get-tuple-element.163), channel_id=1, replica_groups=mesh['parts'=2,'seq'=16] {'seq'}, dimensions={0}, use_global_device_ids=true | all-gather | bytes 139264 | tf_op jit(solution)/shard_map/all_gather | solution.py:101
  178.7 6.9 %reshape.1959 = bf16[4096,4,128]{2,1,0:T(4,128)(2,1)} reshape(bf16[1,4096,512]{2,1,0:T(8,128)(2,1)} %param.23) | data formatting | bytes 8388608 | tf_op jit(solution)/shard_map/reshape.285
  199.0 5.1 %fusion.125 = (f32[4,4,8]{2,0,1:T(4,128)S(1)}, f32[1,4,4,8,4096]{4,3,1,2,0:T(8,128)}) fusion(bf16[4096,4,128,1]{2,1,0,3:T(4,128)(2,1)} %bitcast.281, pred[4096]{0:T(1024)(128)(4,1)S(1)} %iota_compare_fusion, bf16[4,4,8,64]{3,2,1,0:T(8,128)(2,1)S(1)} %bitcast.297, bf16[4,4,8,64]{3,2,1,0:T(8,128)(2,1)S(1)} %bitcast.295), kind=kOutput, calls=%fused_computation.295 | convolution fusion | flops 135856000 | bytes 6328832 | tf_op jit(solution)/shard_map/rtkgd,rpkd->rtkgp/dot_general | solution.py:136
  205.6 3.5 %all-to-all-start = ((f32[16,1,1,32]{3,2,1,0:T(1,128)}), f32[16,1,1,32]{3,2,1,0:T(1,128)S(1)}, u32[]{:S(2)}, u32[]{:S(2)}) async-start(f32[16,1,1,32]{3,2,1,0:T(1,128)} %copy.169), calls=%async_computation | async-start | bytes 16384 | tf_op jit(solution)/shard_map/all_to_all | solution.py:117
  209.7 5.8 %all-to-all-done = f32[16,1,1,32]{3,2,1,0:T(1,128)S(1)} async-done(((f32[16,1,1,32]{3,2,1,0:T(1,128)}), f32[16,1,1,32]{3,2,1,0:T(1,128)S(1)}, u32[]{:S(2)}, u32[]{:S(2)}) %all-to-all-start) | async-done | bytes 2080 | tf_op jit(solution)/shard_map/all_to_all | solution.py:117
  220.3 5.0 %all-to-all-done.4 = f32[16,1,1,1,32]{4,3,2,1,0:T(1,128)S(1)} async-done(((f32[16,1,1,1,32]{4,3,2,1,0:T(1,128)}), f32[16,1,1,1,32]{4,3,2,1,0:T(1,128)S(1)}, u32[]{:S(2)}, u32[]{:S(2)}) %all-to-all-start.4) | async-done | bytes 2080 | tf_op jit(solution)/shard_map/all_to_all | solution.py:112
  225.3 3.5 %all-to-all-start.3 = ((f32[16,1,1,32]{3,2,1,0:T(1,128)}), f32[16,1,1,32]{3,2,1,0:T(1,128)S(1)}, u32[]{:S(2)}, u32[]{:S(2)}) async-start(f32[16,1,1,32]{3,2,1,0:T(1,128)} %copy.174), calls=%async_computation.3 | async-start | bytes 16384 | tf_op jit(solution)/shard_map/all_to_all | solution.py:117
  229.4 5.8 %all-to-all-done.3 = f32[16,1,1,32]{3,2,1,0:T(1,128)S(1)} async-done(((f32[16,1,1,32]{3,2,1,0:T(1,128)}), f32[16,1,1,32]{3,2,1,0:T(1,128)S(1)}, u32[]{:S(2)}, u32[]{:S(2)}) %all-to-all-start.3) | async-done | bytes 2080 | tf_op jit(solution)/shard_map/all_to_all | solution.py:117
  239.9 5.1 %all-to-all-done.7 = f32[16,1,1,1,32]{4,3,2,1,0:T(1,128)S(1)} async-done(((f32[16,1,1,1,32]{4,3,2,1,0:T(1,128)}), f32[16,1,1,1,32]{4,3,2,1,0:T(1,128)S(1)}, u32[]{:S(2)}, u32[]{:S(2)}) %all-to-all-start.7) | async-done | bytes 2080 | tf_op jit(solution)/shard_map/all_to_all | solution.py:112
  245.0 3.5 %all-to-all-start.6 = ((f32[16,1,1,32]{3,2,1,0:T(1,128)}), f32[16,1,1,32]{3,2,1,0:T(1,128)S(1)}, u32[]{:S(2)}, u32[]{:S(2)}) async-start(f32[16,1,1,32]{3,2,1,0:T(1,128)} %copy.179), calls=%async_computation.6 | async-start | bytes 16384 | tf_op jit(solution)/shard_map/all_to_all | solution.py:117
  249.0 6.9 %reshape.1963 = bf16[4096,4,128]{2,1,0:T(4,128)(2,1)} reshape(bf16[1,4096,512]{2,1,0:T(8,128)(2,1)} %param.24) | data formatting | bytes 8388608 | tf_op jit(solution)/shard_map/reshape.300
  256.0 6.0 %all-to-all-start.10 = ((f32[16,1,1,1,32]{4,3,2,1,0:T(1,128)}), f32[16,1,1,1,32]{4,3,2,1,0:T(1,128)S(1)}, u32[]{:S(2)}, u32[]{:S(2)}) async-start(f32[16,1,1,1,32]{4,3,2,1,0:T(1,128)} %constant_dynamic-update-slice_fusion.48), calls=%async_computation.10 | async-start | bytes 16384 | tf_op jit(solution)/shard_map/all_to_all | solution.py:112
  262.0 3.7 %fusion.3 = f32[4,4,8,128]{3,2,1,0:T(8,128)S(1)} fusion(bf16[4096,4,128,1]{2,1,0,3:T(4,128)(2,1)} %bitcast.282, f32[1,4,4,8,4096]{4,3,1,2,0:T(8,128)} %get-tuple-element.181, f32[4,4,8]{2,0,1:T(4,128)S(1)} %max.48), kind=kOutput, calls=%fused_computation.4 | convolution fusion | flops 135266304 | bytes 6357504 | tf_op jit(solution)/shard_map/rtkgp,rpkd->rtkgd/dot_general | solution.py:153
  268.4 4.0 %all-to-all-start.9 = ((f32[16,1,1,32]{3,2,1,0:T(1,128)}), f32[16,1,1,32]{3,2,1,0:T(1,128)S(1)}, u32[]{:S(2)}, u32[]{:S(2)}) async-start(f32[16,1,1,32]{3,2,1,0:T(1,128)} %copy.184), calls=%async_computation.9 | async-start | bytes 16384 | tf_op jit(solution)/shard_map/all_to_all | solution.py:117
  275.2 3.5 %all-to-all-done.9 = f32[16,1,1,32]{3,2,1,0:T(1,128)S(1)} async-done(((f32[16,1,1,32]{3,2,1,0:T(1,128)}), f32[16,1,1,32]{3,2,1,0:T(1,128)S(1)}, u32[]{:S(2)}, u32[]{:S(2)}) %all-to-all-start.9) | async-done | bytes 2080 | tf_op jit(solution)/shard_map/all_to_all | solution.py:117
  278.7 3.5 %all-to-all-start.2 = ((f32[16,1,1,4096]{3,1,2,0:T(1,128)}), f32[16,1,1,4096]{3,1,2,0:T(1,128)S(1)}, u32[]{:S(2)}, u32[]{:S(2)}) async-start(f32[16,1,1,4096]{3,1,2,0:T(1,128)} %bitcast.18), calls=%async_computation.2 | async-start | bytes 524288 | tf_op jit(solution)/shard_map/all_to_all | solution.py:110
  285.3 7.0 %all-to-all-done.2 = f32[16,1,1,4096]{3,1,2,0:T(1,128)S(1)} async-done(((f32[16,1,1,4096]{3,1,2,0:T(1,128)}), f32[16,1,1,4096]{3,1,2,0:T(1,128)S(1)}, u32[]{:S(2)}, u32[]{:S(2)}) %all-to-all-start.2) | async-done | bytes 262176 | tf_op jit(solution)/shard_map/all_to_all | solution.py:110
  292.2 3.5 %all-to-all-start.5 = ((f32[16,1,1,4096]{3,1,2,0:T(1,128)}), f32[16,1,1,4096]{3,1,2,0:T(1,128)S(1)}, u32[]{:S(2)}, u32[]{:S(2)}) async-start(f32[16,1,1,4096]{3,1,2,0:T(1,128)} %bitcast.33), calls=%async_computation.5 | async-start | bytes 524288 | tf_op jit(solution)/shard_map/all_to_all | solution.py:110
  296.5 9.3 %all-to-all-done.5 = f32[16,1,1,4096]{3,1,2,0:T(1,128)S(1)} async-done(((f32[16,1,1,4096]{3,1,2,0:T(1,128)}), f32[16,1,1,4096]{3,1,2,0:T(1,128)S(1)}, u32[]{:S(2)}, u32[]{:S(2)}) %all-to-all-start.5) | async-done | bytes 262176 | tf_op jit(solution)/shard_map/all_to_all | solution.py:110
  305.8 3.5 %all-to-all-start.8 = ((f32[16,1,1,4096]{3,1,2,0:T(1,128)}), f32[16,1,1,4096]{3,1,2,0:T(1,128)S(1)}, u32[]{:S(2)}, u32[]{:S(2)}) async-start(f32[16,1,1,4096]{3,1,2,0:T(1,128)} %bitcast.47), calls=%async_computation.8 | async-start | bytes 524288 | tf_op jit(solution)/shard_map/all_to_all | solution.py:110
  310.8 8.6 %all-to-all-done.8 = f32[16,1,1,4096]{3,1,2,0:T(1,128)S(1)} async-done(((f32[16,1,1,4096]{3,1,2,0:T(1,128)}), f32[16,1,1,4096]{3,1,2,0:T(1,128)S(1)}, u32[]{:S(2)}, u32[]{:S(2)}) %all-to-all-start.8) | async-done | bytes 262176 | tf_op jit(solution)/shard_map/all_to_all | solution.py:110
  319.3 3.5 %all-to-all-start.11 = ((f32[16,1,1,4096]{3,1,2,0:T(1,128)}), f32[16,1,1,4096]{3,1,2,0:T(1,128)S(1)}, u32[]{:S(2)}, u32[]{:S(2)}) async-start(f32[16,1,1,4096]{3,1,2,0:T(1,128)} %bitcast.61), calls=%async_computation.11 | async-start | bytes 524288 | tf_op jit(solution)/shard_map/all_to_all | solution.py:110
  324.2 8.7 %all-to-all-done.11 = f32[16,1,1,4096]{3,1,2,0:T(1,128)S(1)} async-done(((f32[16,1,1,4096]{3,1,2,0:T(1,128)}), f32[16,1,1,4096]{3,1,2,0:T(1,128)S(1)}, u32[]{:S(2)}, u32[]{:S(2)}) %all-to-all-start.11) | async-done | bytes 262176 | tf_op jit(solution)/shard_map/all_to_all | solution.py:110
  (305 shorter events, 109.2 us)
Async XLA Ops:
  0.0 27.2 %copy-start = (bf16[1920,512]{1,0:T(8,128)(2,1)S(1)}, bf16[1920,512]{1,0:T(8,128)(2,1)}, u32[]{:S(2)}) copy-start(bf16[1920,512]{1,0:T(8,128)(2,1)} %param.16) | copy-start | bytes 5898244
  51.9 17.3 %copy-start.39 = (bf16[512,512]{1,0:T(8,128)(2,1)S(1)}, bf16[512,512]{1,0:T(8,128)(2,1)}, u32[]{:S(2)}) copy-start(bf16[512,512]{1,0:T(8,128)(2,1)} %param.19) | copy-start | bytes 1572868
  62.2 143.5 %all-to-all-start.1 = ((f32[16,1,1,1,32]{4,3,2,1,0:T(1,128)}), f32[16,1,1,1,32]{4,3,2,1,0:T(1,128)S(1)}, u32[]{:S(2)}, u32[]{:S(2)}) async-start(f32[16,1,1,1,32]{4,3,2,1,0:T(1,128)} %constant_dynamic-update-slice_fusion), calls=%async_computation.1 | async-start | bytes 16384 | tf_op jit(solution)/shard_map/all_to_all | solution.py:112
  110.1 19.8 %copy-start.3 = (bf16[1920,4,128,1]{2,0,3,1:T(8,128)(2,1)S(1)}, bf16[1920,4,128,1]{2,0,3,1:T(8,128)(2,1)}, u32[]{:S(2)}) copy-start(bf16[1920,4,128,1]{2,0,3,1:T(8,128)(2,1)} %copy-done.2) | copy-start | bytes 5898244
  145.5 25.5 %copy-start.12 = (f32[16,4,8]{0,2,1:T(8,128)}, f32[16,4,8]{0,2,1:T(8,128)S(1)}, u32[]{:S(2)}) copy-start(f32[16,4,8]{0,2,1:T(8,128)S(1)} %fusion.15) | copy-start | bytes 6148
  178.6 15.2 %copy-start.33 = (f32[1,1,1,1,32]{4,3,2,1,0:T(1,128)S(1)}, f32[1,1,1,1,32]{4,3,2,1,0:T(1,128)}, u32[]{:S(2)}) copy-start(f32[1,1,1,1,32]{4,3,2,1,0:T(1,128)} %stack.244) | copy-start | bytes 388
  178.6 15.2 %copy-start.32 = (f32[1,1,1,1,32]{4,3,2,1,0:T(1,128)S(1)}, f32[1,1,1,1,32]{4,3,2,1,0:T(1,128)}, u32[]{:S(2)}) copy-start(f32[1,1,1,1,32]{4,3,2,1,0:T(1,128)} %stack.245) | copy-start | bytes 388
  178.6 15.2 %copy-start.31 = (f32[1,1,1,1,32]{4,3,2,1,0:T(1,128)S(1)}, f32[1,1,1,1,32]{4,3,2,1,0:T(1,128)}, u32[]{:S(2)}) copy-start(f32[1,1,1,1,32]{4,3,2,1,0:T(1,128)} %stack.246) | copy-start | bytes 388
  178.6 15.3 %copy-start.30 = (f32[1,1,1,1,32]{4,3,2,1,0:T(1,128)S(1)}, f32[1,1,1,1,32]{4,3,2,1,0:T(1,128)}, u32[]{:S(2)}) copy-start(f32[1,1,1,1,32]{4,3,2,1,0:T(1,128)} %stack.247) | copy-start | bytes 388
  178.7 15.3 %copy-start.29 = (f32[1,1,1,1,32]{4,3,2,1,0:T(1,128)S(1)}, f32[1,1,1,1,32]{4,3,2,1,0:T(1,128)}, u32[]{:S(2)}) copy-start(f32[1,1,1,1,32]{4,3,2,1,0:T(1,128)} %stack.248) | copy-start | bytes 388
  178.7 15.3 %copy-start.28 = (f32[1,1,1,1,32]{4,3,2,1,0:T(1,128)S(1)}, f32[1,1,1,1,32]{4,3,2,1,0:T(1,128)}, u32[]{:S(2)}) copy-start(f32[1,1,1,1,32]{4,3,2,1,0:T(1,128)} %stack.249) | copy-start | bytes 388
  178.7 15.3 %copy-start.27 = (f32[1,1,1,1,32]{4,3,2,1,0:T(1,128)S(1)}, f32[1,1,1,1,32]{4,3,2,1,0:T(1,128)}, u32[]{:S(2)}) copy-start(f32[1,1,1,1,32]{4,3,2,1,0:T(1,128)} %stack.250) | copy-start | bytes 388
  178.7 15.3 %copy-start.26 = (f32[1,1,1,1,32]{4,3,2,1,0:T(1,128)S(1)}, f32[1,1,1,1,32]{4,3,2,1,0:T(1,128)}, u32[]{:S(2)}) copy-start(f32[1,1,1,1,32]{4,3,2,1,0:T(1,128)} %stack.251) | copy-start | bytes 388
  178.7 15.3 %copy-start.24 = (f32[1,1,1,1,32]{4,3,2,1,0:T(1,128)S(1)}, f32[1,1,1,1,32]{4,3,2,1,0:T(1,128)}, u32[]{:S(2)}) copy-start(f32[1,1,1,1,32]{4,3,2,1,0:T(1,128)} %stack.252) | copy-start | bytes 388
  178.7 15.3 %copy-start.25 = (f32[1,1,1,1,32]{4,3,2,1,0:T(1,128)S(1)}, f32[1,1,1,1,32]{4,3,2,1,0:T(1,128)}, u32[]{:S(2)}) copy-start(f32[1,1,1,1,32]{4,3,2,1,0:T(1,128)} %stack.253) | copy-start | bytes 388
  185.7 18.4 %copy-start.42 = (pred[4,4]{1,0:T(4,128)(4,1)S(1)}, pred[4,4]{1,0:T(4,128)(4,1)}, u32[]{:S(2)}) copy-start(pred[4,4]{1,0:T(4,128)(4,1)} %iota_compare_fusion.1) | copy-start | bytes 52
  185.7 33.9 %copy-start.11 = (f32[16,4,8]{0,2,1:T(8,128)S(1)}, f32[16,4,8]{0,2,1:T(8,128)}, u32[]{:S(2)}) copy-start(f32[16,4,8]{0,2,1:T(8,128)} %copy-done.10) | copy-start | bytes 6148
  185.7 53.5 %copy-start.13 = (f32[16,4,8]{0,2,1:T(8,128)S(1)}, f32[16,4,8]{0,2,1:T(8,128)}, u32[]{:S(2)}) copy-start(f32[16,4,8]{0,2,1:T(8,128)} %copy-done.12) | copy-start | bytes 6148
  205.6 9.9 %all-to-all-start = ((f32[16,1,1,32]{3,2,1,0:T(1,128)}), f32[16,1,1,32]{3,2,1,0:T(1,128)S(1)}, u32[]{:S(2)}, u32[]{:S(2)}) async-start(f32[16,1,1,32]{3,2,1,0:T(1,128)} %copy.169), calls=%async_computation | async-start | bytes 16384 | tf_op jit(solution)/shard_map/all_to_all | solution.py:117
  215.5 9.8 %all-to-all-start.4 = ((f32[16,1,1,1,32]{4,3,2,1,0:T(1,128)}), f32[16,1,1,1,32]{4,3,2,1,0:T(1,128)S(1)}, u32[]{:S(2)}, u32[]{:S(2)}) async-start(f32[16,1,1,1,32]{4,3,2,1,0:T(1,128)} %constant_dynamic-update-slice_fusion.16), calls=%async_computation.4 | async-start | bytes 16384 | tf_op jit(solution)/shard_map/all_to_all | solution.py:112
  225.3 9.9 %all-to-all-start.3 = ((f32[16,1,1,32]{3,2,1,0:T(1,128)}), f32[16,1,1,32]{3,2,1,0:T(1,128)S(1)}, u32[]{:S(2)}, u32[]{:S(2)}) async-start(f32[16,1,1,32]{3,2,1,0:T(1,128)} %copy.174), calls=%async_computation.3 | async-start | bytes 16384 | tf_op jit(solution)/shard_map/all_to_all | solution.py:117
  235.2 9.8 %all-to-all-start.7 = ((f32[16,1,1,1,32]{4,3,2,1,0:T(1,128)}), f32[16,1,1,1,32]{4,3,2,1,0:T(1,128)S(1)}, u32[]{:S(2)}, u32[]{:S(2)}) async-start(f32[16,1,1,1,32]{4,3,2,1,0:T(1,128)} %copy-done.14), calls=%async_computation.7 | async-start | bytes 16384 | tf_op jit(solution)/shard_map/all_to_all | solution.py:112
  245.0 11.0 %all-to-all-start.6 = ((f32[16,1,1,32]{3,2,1,0:T(1,128)}), f32[16,1,1,32]{3,2,1,0:T(1,128)S(1)}, u32[]{:S(2)}, u32[]{:S(2)}) async-start(f32[16,1,1,32]{3,2,1,0:T(1,128)} %copy.179), calls=%async_computation.6 | async-start | bytes 16384 | tf_op jit(solution)/shard_map/all_to_all | solution.py:117
  256.0 29.3 %copy-start.8 = (f32[16,1,1,32]{3,2,1,0:T(1,128)}, f32[16,1,1,32]{3,2,1,0:T(1,128)S(1)}, u32[]{:S(2)}) copy-start(f32[16,1,1,32]{3,2,1,0:T(1,128)S(1)} %all-to-all-done.6) | copy-start | bytes 6148
  256.0 12.4 %all-to-all-start.10 = ((f32[16,1,1,1,32]{4,3,2,1,0:T(1,128)}), f32[16,1,1,1,32]{4,3,2,1,0:T(1,128)S(1)}, u32[]{:S(2)}, u32[]{:S(2)}) async-start(f32[16,1,1,1,32]{4,3,2,1,0:T(1,128)} %constant_dynamic-update-slice_fusion.48), calls=%async_computation.10 | async-start | bytes 16384 | tf_op jit(solution)/shard_map/all_to_all | solution.py:112
  265.7 19.2 %copy-start.16 = (bf16[1,4,512]{2,1,0:T(4,128)(2,1)S(1)}, bf16[1,4,512]{2,1,0:T(4,128)(2,1)}, u32[]{:S(2)}) copy-start(bf16[1,4,512]{2,1,0:T(4,128)(2,1)} %param.22) | copy-start | bytes 12292
  268.4 10.3 %all-to-all-start.9 = ((f32[16,1,1,32]{3,2,1,0:T(1,128)}), f32[16,1,1,32]{3,2,1,0:T(1,128)S(1)}, u32[]{:S(2)}, u32[]{:S(2)}) async-start(f32[16,1,1,32]{3,2,1,0:T(1,128)} %copy.184), calls=%async_computation.9 | async-start | bytes 16384 | tf_op jit(solution)/shard_map/all_to_all | solution.py:117
  278.7 13.5 %all-to-all-start.2 = ((f32[16,1,1,4096]{3,1,2,0:T(1,128)}), f32[16,1,1,4096]{3,1,2,0:T(1,128)S(1)}, u32[]{:S(2)}, u32[]{:S(2)}) async-start(f32[16,1,1,4096]{3,1,2,0:T(1,128)} %bitcast.18), calls=%async_computation.2 | async-start | bytes 524288 | tf_op jit(solution)/shard_map/all_to_all | solution.py:110
  282.2 52.2 %copy-start.1 = (bf16[1920,512]{1,0:T(8,128)(2,1)S(1)}, bf16[1920,512]{1,0:T(8,128)(2,1)}, u32[]{:S(2)}) copy-start(bf16[1920,512]{1,0:T(8,128)(2,1)} %param.16) | copy-start | bytes 5898244
  292.2 13.5 %all-to-all-start.5 = ((f32[16,1,1,4096]{3,1,2,0:T(1,128)}), f32[16,1,1,4096]{3,1,2,0:T(1,128)S(1)}, u32[]{:S(2)}, u32[]{:S(2)}) async-start(f32[16,1,1,4096]{3,1,2,0:T(1,128)} %bitcast.33), calls=%async_computation.5 | async-start | bytes 524288 | tf_op jit(solution)/shard_map/all_to_all | solution.py:110
  305.8 13.5 %all-to-all-start.8 = ((f32[16,1,1,4096]{3,1,2,0:T(1,128)}), f32[16,1,1,4096]{3,1,2,0:T(1,128)S(1)}, u32[]{:S(2)}, u32[]{:S(2)}) async-start(f32[16,1,1,4096]{3,1,2,0:T(1,128)} %bitcast.47), calls=%async_computation.8 | async-start | bytes 524288 | tf_op jit(solution)/shard_map/all_to_all | solution.py:110
  319.3 13.5 %all-to-all-start.11 = ((f32[16,1,1,4096]{3,1,2,0:T(1,128)}), f32[16,1,1,4096]{3,1,2,0:T(1,128)S(1)}, u32[]{:S(2)}, u32[]{:S(2)}) async-start(f32[16,1,1,4096]{3,1,2,0:T(1,128)} %bitcast.61), calls=%async_computation.11 | async-start | bytes 524288 | tf_op jit(solution)/shard_map/all_to_all | solution.py:110
  (23 other events, 177.5 us)
